TPU v7x, 32 devices: a whole 2x2x4 slice. The times are simulated.
32 devices in a mesh: grp: 4 (over z), dev: 8 (over y, x, core).
Axes of the slice: x: 2, y: 2, z: 4, core: 2. Of those that a mesh axis runs over, the one named last changes fastest.
Arguments:
- omega: float32 [4, 32, 256, 128], P('grp', 'dev'), may hold values from -6 to 6
- u_factor: float32 [4, 32, 80, 256, 32], P('grp', 'dev'), may hold values from -0.0625 to 0.0625
- v_factor: float32 [4, 32, 80, 256, 32], P('grp', 'dev'), may hold values from -0.375 to 0.375
- columns: int32 [4, 32, 80, 1], P('grp', 'dev'), may hold values from 0 to 31; in each aligned block of 320 rows (0 to 319, 320 to 639, ..., all dimensions but the last counted through in order) at most 11 rows name the same one
- ranks: int32 [4, 32, 80], P('grp', 'dev'), may hold values from 8 to 32
Outputs:
- leaf_basis: float32 [32, 256, 128], P('dev', 'grp')
- transfer: float32 [32, 256, 128], P('dev')
Inputs may be any that keep to these rules, and one draw needn't show every extreme that they name: `columns`: within the 320 blocks of one device's row clusters in one group, at most 11 name any one column cluster, and some column cluster is named by exactly 11.
All inputs are finite; a program needn't handle non-finite values.
Results may differ from a plain program's by a relative error of at most 0.0003.
Values sent between devices are 32-bit elements; how exact they have to be, the bound alone decides.
No kernel may reach another device: no remote copies, remote signals or barrier semaphores. Data moves between devices by JAX's collectives and lax.ppermute only.
A program may use at most 192 MiB of HBM per device.

v0:
```python
import jax
import jax.numpy as jnp
from jax import lax
from jax.sharding import PartitionSpec as P

precise = lax.Precision.HIGHEST


def swapped(value, axis, apart):
    mask = 2**apart
    pairs = [(source, source ^ mask) for source in range(lax.axis_size(axis))]
    return lax.ppermute(value, axis, pairs)


def on_device(omega, u_factor, v_factor, columns, ranks):
    n_local = u_factor.shape[1]
    n_blocks = u_factor.shape[2]
    leaf_rows = u_factor.shape[3]
    rank_width = u_factor.shape[4]
    probe_count = omega.shape[3]
    dev_count = lax.axis_size("dev")
    grp_count = lax.axis_size("grp")
    col_flat = columns[0, :, :, 0].reshape(n_local * n_blocks)
    v_flat = v_factor[0].reshape(n_local * n_blocks, leaf_rows, rank_width)
    whole_probe = lax.all_gather(omega, "dev", axis=1, tiled=True)[0]
    coeff = jnp.einsum("bik,bip->bkp", v_flat, whole_probe[col_flat], precision=precise)
    rank_mask = (
        jnp.arange(rank_width, dtype=jnp.int32)[None, None, :] < ranks[0][:, :, None]
    ).astype(jnp.float32)
    masked_rows = u_factor[0] * rank_mask[:, :, None, :]
    partial_sketch = jnp.einsum(
        "cbik,cbkp->cip",
        masked_rows,
        coeff.reshape(n_local, n_blocks, rank_width, probe_count),
        precision=precise,
    )
    quarter = leaf_rows // grp_count
    total_sketch = lax.psum(partial_sketch, "grp")
    gram_matrix = jnp.einsum("cip,ciq->cpq", total_sketch, total_sketch, precision=precise)
    own_rows = lax.dynamic_slice_in_dim(total_sketch, lax.axis_index("grp") * quarter, quarter, 1)
    pair_gram = gram_matrix[0::2] + gram_matrix[1::2]
    top_gram = pair_gram[0] + pair_gram[1]
    device_index = lax.axis_index("dev")
    tree_bits = dev_count.bit_length() - 1
    identity = jnp.eye(probe_count, dtype=jnp.float32)
    keep_left = identity
    keep_right = identity
    owned = device_index < 0
    current = top_gram
    for depth_step in range(tree_bits):
        sibling = swapped(current, "dev", depth_step)
        is_left = device_index // 2**depth_step % 2 == 0
        left_gram = jnp.where(is_left, current, sibling)
        right_gram = jnp.where(is_left, sibling, current)
        owner = device_index % 2 ** (depth_step + 1) == 2**depth_step - 1
        keep_left = jnp.where(owner, left_gram, keep_left)
        keep_right = jnp.where(owner, right_gram, keep_right)
        owned = jnp.logical_or(owned, owner)
        current = left_gram + right_gram
    all_grams = jnp.concatenate(
        [
            gram_matrix,
            pair_gram,
            top_gram[None],
            keep_left[None],
            keep_right[None],
            (keep_left + keep_right)[None],
        ],
        axis=0,
    )
    all_lower = jnp.linalg.cholesky(all_grams)
    all_upper = jnp.swapaxes(all_lower, 1, 2)
    leaf_basis = lax.linalg.triangular_solve(
        all_lower[0:4], own_rows, left_side=False, lower=True, transpose_a=True
    )
    left_parts = jnp.stack([all_upper[0], all_upper[2], all_upper[4], all_upper[7]], axis=0)
    right_parts = jnp.stack([all_upper[1], all_upper[3], all_upper[5], all_upper[8]], axis=0)
    parent_lower = jnp.stack([all_lower[4], all_lower[5], all_lower[6], all_lower[9]], axis=0)
    stacked_rows = jnp.concatenate([left_parts, right_parts], axis=1)
    node_transfer = lax.linalg.triangular_solve(
        parent_lower, stacked_rows, left_side=False, lower=True, transpose_a=True
    )
    kept = jnp.where(owned, node_transfer[3], jnp.zeros_like(node_transfer[3]))
    transfer = jnp.stack([node_transfer[0], node_transfer[1], node_transfer[2], kept], axis=0)
    return (leaf_basis, transfer)


def solution(mesh):
    placed = (
        P("grp", "dev", None, None),
        P("grp", "dev", None, None, None),
        P("grp", "dev", None, None, None),
        P("grp", "dev", None, None),
        P("grp", "dev", None),
    )
    return jax.shard_map(
        on_device,
        mesh=mesh,
        in_specs=placed,
        out_specs=(P("dev", "grp", None), P("dev", None, None)),
        check_vma=False,
    )
```

profile of v0, /device:TPU:0, one launch (start us, length us, event | category | flops | bytes accessed | tf_op | source)
XLA Modules:
  0.0 378.8 jit_solution(2373997758977308243)
XLA Ops:
  7.2 0.0 all-gather.2.cloned.1.call-start
  7.2 0.7 all-gather.2.cloned.1.call-update
  7.9 0.0 all-reduce.2.cloned.1.call-start
  7.9 0.5 broadcast.113
  8.5 1.3 reduce.11
  9.8 0.1 reshape_squeeze.6
  9.9 0.8 fusion.24
  10.7 38.5 %all-gather.2.cloned.1.call-done = f32[1,32,256,128]{3,2,0,1:T(8,128)} async-done(((f32[1,4,256,128]{3,2,0,1:T(8,128)}), f32[1,32,256,128]{3,2,0,1:T(8,128)}) %all-gather.2.cloned.1.call-update) | async-done | bytes 4194320 | tf_op jit(solution)/shard_map/all_gather | solution.py:25
  49.2 19.8 %gather_fusion = f32[320,256,128]{2,1,0:T(8,128)} fusion(f32[32,256,128]{2,1,0:T(8,128)} %bitcast.51, s32[1024]{0:T(1024)S(1)} %pad_clamp_fusion), kind=kCustom, calls=%fused_computation | custom fusion | bytes 83887360 | tf_op jit(solution)/shard_map/gather | solution.py:26
  69.0 0.0 copy-start
  69.0 31.7 %fusion.40 = f32[320,128,32]{1,2,0:T(8,128)S(1)} fusion(f32[320,256,128]{2,1,0:T(8,128)} %gather_fusion, f32[320,256,32]{1,2,0:T(8,128)} %bitcast.52), kind=kOutput, calls=%fused_computation.68 | convolution fusion | flops 4026531840 | bytes 57671680 | tf_op jit(solution)/shard_map/bik,bip->bkp/dot_general | solution.py:26
  100.6 0.0 copy-done
  100.7 18.9 %fusion.2 = f32[4,256,128]{2,1,0:T(8,128)} fusion(f32[4,80,32,128]{3,2,1,0:T(8,128)S(1)} %bitcast.53, f32[1,4,80,256,32]{3,4,2,1,0:T(8,128)S(1)} %copy-done, f32[4,80,32]{2,1,0:T(8,128)S(1)} %fusion.24), kind=kOutput, calls=%fused_computation.4 | convolution fusion | flops 4029153280 | bytes 16293888 | tf_op jit(solution)/shard_map/cbik,cbkp->cip/dot_general | solution.py:31
  119.6 0.0 all-reduce.2.cloned.1.call-update
  119.6 38.9 %all-reduce.2.cloned.1.call-done = f32[4,256,128]{2,1,0:T(8,128)} async-done(((f32[4,256,128]{2,1,0:T(8,128)}), f32[4,256,128]{2,1,0:T(8,128)}) %all-reduce.2.cloned.1.call-update) | async-done | bytes 524304 | tf_op jit(solution)/shard_map/psum | solution.py:38
  158.4 2.2 constant_dynamic-update-slice_fusion.1
  160.7 0.1 collective-permute-start
  160.9 1.2 collective-permute-done
  162.1 1.5 collective-permute-start.1
  163.6 0.1 copy.35
  163.8 2.6 collective-permute-done.1
  166.4 1.5 collective-permute-start.2
  168.0 2.8 collective-permute-done.2
  170.9 0.2 copy.40
  171.1 0.1 fusion.3
  171.2 117.2 %custom-call.10 = f32[10,128,128]{2,1,0:T(8,128)S(1)} custom-call(f32[10,128,128]{2,1,0:T(8,128)S(1)} %fusion.3), custom_call_target="Cholesky" | custom-call | tf_op jit(solution)/shard_map/jit(cholesky)/cholesky | solution.py:71
  288.4 0.1 select_reduce_fusion
  288.5 0.1 compare_reduce_fusion
  288.6 0.1 select_select_fusion
  288.7 0.1 fusion.46
  288.9 39.5 %custom-call.11 = f32[4,1,128,128]{2,3,1,0:T(8,128)S(1)} custom-call(f32[4,1,128,128]{3,2,1,0:T(8,128)S(1)} %fusion.20), custom_call_target="InvertDiagBlocksLowerTriangular" | custom-call | tf_op jit(solution)/shard_map/triangular_solve | solution.py:73
  328.5 39.3 %custom-call.12 = f32[4,1,128,128]{2,3,1,0:T(8,128)S(1)} custom-call(f32[4,1,128,128]{3,2,1,0:T(8,128)S(1)} %maximum_select_fusion), custom_call_target="InvertDiagBlocksLowerTriangular" | custom-call | tf_op jit(solution)/shard_map/triangular_solve | solution.py:80
  367.9 1.0 fusion.4
  369.0 0.8 pad_maximum_fusion
  369.8 1.9 fusion.22
  (18 shorter events, 0.4 us)
Async XLA Ops:
  7.2 42.0 %all-gather.2.cloned.1.call-start = ((), (), s32[]{:S(2)}) async-start(), calls=%async_computation | async-start | bytes 4718592 | tf_op jit(solution)/shard_map/all_gather | solution.py:25
  7.9 150.5 %all-reduce.2.cloned.1.call-start = ((), (), s32[]{:S(2)}) async-start(), calls=%async_computation.1 | async-start | bytes 1048576 | tf_op jit(solution)/shard_map/psum | solution.py:38
  69.0 31.7 %copy-start = (f32[1,4,80,256,32]{3,4,2,1,0:T(8,128)S(1)}, f32[1,4,80,256,32]{3,4,2,1,0:T(8,128)}, u32[]{:S(2)}) copy-start(f32[1,4,80,256,32]{3,4,2,1,0:T(8,128)} %param.6) | copy-start | bytes 31457284
  160.7 1.3 collective-permute-start
  162.1 4.3 %collective-permute-start.1 = (f32[128,128]{0,1:T(8,128)S(1)}, f32[128,128]{0,1:T(8,128)S(1)}, u32[]{:S(2)}, u32[]{:S(2)}) collective-permute-start(f32[128,128]{0,1:T(8,128)S(1)} %fusion.30), channel_id=1, source_target_pairs={{0,2},{1,3},{2,0},{3,1},{4,6},{5,7},{6,4},{7,5},{8,10},{9,11},{10,... | collective-permute-start | bytes 196616 | tf_op jit(solution)/shard_map/ppermute | solution.py:12
  166.4 4.3 %collective-permute-start.2 = (f32[128,128]{0,1:T(8,128)S(1)}, f32[128,128]{0,1:T(8,128)S(1)}, u32[]{:S(2)}, u32[]{:S(2)}) collective-permute-start(f32[128,128]{0,1:T(8,128)S(1)} %fusion.31), channel_id=1, source_target_pairs={{0,4},{1,5},{2,6},{3,7},{4,0},{5,1},{6,2},{7,3},{8,12},{9,13},{10,... | collective-permute-start | bytes 196616 | tf_op jit(solution)/shard_map/ppermute | solution.py:12
Sparse Core Ops, SparseCore 0:
  9.9 39.2 all-gather.1
  119.7 38.6 all-reduce.1
where the time goes:
time: 385 us; the launch traced here: 379 us
  other arithmetic  200 us (52%)
  waiting for transfers between devices  84.6 us (22%)
  matrix products  55.8 us (14%)
  local copies, waits for them, and re-layouts  20.8 us (5%)
  between operations  14.6 us (4%)
    another operation x4, other arithmetic, on_device(): all_lower = jnp.linalg.cholesky(all_grams)  117 us
    another operation x3, other arithmetic, on_device(): lax.linalg.triangular_solve(all_lower[0:4], own_rows, left_side=False, lo...  39.6 us
    another operation x2, other arithmetic, on_device(): lax.linalg.triangular_solve(parent_lower, stacked_rows, left_side=False,...  39.3 us
    psum x1, waiting for transfers between devices, on_device(): total_sketch = lax.psum(partial_sketch, 'grp')  38.9 us
    all_gather x1, waiting for transfers between devices, on_device(): whole_probe = lax.all_gather(omega, 'dev', axis=1, tiled=True)[0]  38.5 us
    dot_general x1, matrix products, on_device(): jnp.einsum('bik,bip->bkp', v_flat, whole_probe[col_flat], precision=precise)  31.7 us
    gather x1, local copies, waits for them, and re-layouts, on_device(): whole_probe[col_flat]  19.8 us
    dot_general x1, matrix products, on_device(): jnp.einsum('cbik,cbkp->cip', masked_rows, coeff.reshape(n_local, n_blocks...  18.9 us
  transfers between devices with their start and end apart: 5, of which 5 were waited for; matrix products, arithmetic and copies ran while one was open for 1% of the time, Pallas kernels for 0%

commit v1 on v0

--- a/solution.py
+++ b/solution.py
@@ -35,7 +35,7 @@
         precision=precise,
     )
     quarter = leaf_rows // grp_count
-    total_sketch = lax.psum(partial_sketch, "grp")
+    total_sketch = jnp.sum(lax.all_gather(partial_sketch, "grp"), axis=0)
     gram_matrix = jnp.einsum("cip,ciq->cpq", total_sketch, total_sketch, precision=precise)
     own_rows = lax.dynamic_slice_in_dim(total_sketch, lax.axis_index("grp") * quarter, quarter, 1)
     pair_gram = gram_matrix[0::2] + gram_matrix[1::2]

time: 385 us -> 391 us (1.016)
  waiting for transfers between devices: 84.6 us -> 91.6 us
    all_gather x0 -> x1, waiting for transfers between devices: none -> 45.8 us  [on_device(): total_sketch = jnp.sum(lax.all_gather(partial_sketch, 'grp'), axis=0)]
    psum x1 -> x0, waiting for transfers between devices: 38.9 us -> none  [on_device(): total_sketch = lax.psum(partial_sketch, 'grp')]
where the time goes in v1:
time: 391 us; the launch traced here: 385 us
  other arithmetic  202 us (52%)
  waiting for transfers between devices  91.6 us (23%)
  matrix products  53.7 us (14%)
  local copies, waits for them, and re-layouts  20.8 us (5%)
  between operations  14.6 us (4%)
    another operation x4, other arithmetic, on_device(): all_lower = jnp.linalg.cholesky(all_grams)  117 us
    all_gather x1, waiting for transfers between devices, on_device(): total_sketch = jnp.sum(lax.all_gather(partial_sketch, 'grp'), axis=0)  45.8 us
    another operation x3, other arithmetic, on_device(): lax.linalg.triangular_solve(all_lower[0:4], own_rows, left_side=False, lo...  39.6 us
    another operation x2, other arithmetic, on_device(): lax.linalg.triangular_solve(parent_lower, stacked_rows, left_side=False,...  39.3 us
    all_gather x1, waiting for transfers between devices, on_device(): whole_probe = lax.all_gather(omega, 'dev', axis=1, tiled=True)[0]  38.5 us
    dot_general x1, matrix products, on_device(): jnp.einsum('bik,bip->bkp', v_flat, whole_probe[col_flat], precision=precise)  31.7 us
    gather x1, local copies, waits for them, and re-layouts, on_device(): whole_probe[col_flat]  19.8 us
    dot_general x1, matrix products, on_device(): jnp.einsum('cbik,cbkp->cip', masked_rows, coeff.reshape(n_local, n_blocks...  18.9 us
  transfers between devices with their start and end apart: 5, of which 5 were waited for; matrix products, arithmetic and copies ran while one was open for 1% of the time, Pallas kernels for 0%

profile of v1, /device:TPU:0, one launch (start us, length us, event | category | flops | bytes accessed | tf_op | source)
XLA Modules:
  0.0 385.4 jit_solution(9090890259245305719)
XLA Ops:
  7.2 0.0 all-gather.4.cloned.1.call-start
  7.2 0.7 all-gather.4.cloned.1.call-update
  7.9 0.0 all-gather.6.cloned.1.call-start
  7.9 0.5 broadcast.113
  8.5 1.3 reduce.11
  9.8 0.1 reshape_squeeze.6
  9.9 0.8 fusion.24
  10.7 38.5 %all-gather.4.cloned.1.call-done = f32[1,32,256,128]{3,2,0,1:T(8,128)} async-done(((f32[1,4,256,128]{3,2,0,1:T(8,128)}), f32[1,32,256,128]{3,2,0,1:T(8,128)}) %all-gather.4.cloned.1.call-update) | async-done | bytes 4194320 | tf_op jit(solution)/shard_map/all_gather | solution.py:25
  49.2 19.8 %gather_fusion = f32[320,256,128]{2,1,0:T(8,128)} fusion(f32[32,256,128]{2,1,0:T(8,128)} %bitcast.52, s32[1024]{0:T(1024)S(1)} %pad_clamp_fusion), kind=kCustom, calls=%fused_computation | custom fusion | bytes 83887360 | tf_op jit(solution)/shard_map/gather | solution.py:26
  69.0 0.0 copy-start
  69.0 31.7 %fusion.40 = f32[320,128,32]{1,2,0:T(8,128)S(1)} fusion(f32[320,256,128]{2,1,0:T(8,128)} %gather_fusion, f32[320,256,32]{1,2,0:T(8,128)} %bitcast.53), kind=kOutput, calls=%fused_computation.68 | convolution fusion | flops 4026531840 | bytes 57671680 | tf_op jit(solution)/shard_map/bik,bip->bkp/dot_general | solution.py:26
  100.6 0.0 copy-done
  100.7 18.9 %fusion.2 = f32[4,256,128]{2,1,0:T(8,128)} fusion(f32[4,80,32,128]{3,2,1,0:T(8,128)S(1)} %bitcast.54, f32[1,4,80,256,32]{3,4,2,1,0:T(8,128)S(1)} %copy-done, f32[4,80,32]{2,1,0:T(8,128)S(1)} %fusion.24), kind=kOutput, calls=%fused_computation.4 | convolution fusion | flops 4029153280 | bytes 16293888 | tf_op jit(solution)/shard_map/cbik,cbkp->cip/dot_general | solution.py:31
  119.6 0.0 all-gather.6.cloned.1.call-update
  119.6 45.8 %all-gather.6.cloned.1.call-done = f32[16,256,128]{2,1,0:T(8,128)} async-done(((f32[4,256,128]{2,1,0:T(8,128)}), f32[16,256,128]{2,1,0:T(8,128)}) %all-gather.6.cloned.1.call-update) | async-done | bytes 2097168 | tf_op jit(solution)/shard_map/all_gather | solution.py:38
  165.4 1.8 reduce_sum.9
  167.2 1.0 constant_dynamic-update-slice_fusion.1
  168.3 0.1 collective-permute-start
  168.4 1.2 collective-permute-done
  169.6 1.5 collective-permute-start.1
  171.2 0.1 copy.35
  171.3 2.6 collective-permute-done.1
  174.0 1.5 collective-permute-start.2
  175.5 2.8 collective-permute-done.2
  178.4 0.2 copy.40
  178.6 0.1 fusion.3
  178.7 117.2 %custom-call.10 = f32[10,128,128]{2,1,0:T(8,128)S(1)} custom-call(f32[10,128,128]{2,1,0:T(8,128)S(1)} %fusion.3), custom_call_target="Cholesky" | custom-call | tf_op jit(solution)/shard_map/jit(cholesky)/cholesky | solution.py:71
  295.9 0.1 select_reduce_fusion
  296.0 0.1 compare_reduce_fusion
  296.1 0.1 select_select_fusion
  296.3 0.1 fusion.46
  296.5 39.5 %custom-call.11 = f32[4,1,128,128]{2,3,1,0:T(8,128)S(1)} custom-call(f32[4,1,128,128]{3,2,1,0:T(8,128)S(1)} %fusion.20), custom_call_target="InvertDiagBlocksLowerTriangular" | custom-call | tf_op jit(solution)/shard_map/triangular_solve | solution.py:73
  336.1 39.3 %custom-call.12 = f32[4,1,128,128]{2,3,1,0:T(8,128)S(1)} custom-call(f32[4,1,128,128]{3,2,1,0:T(8,128)S(1)} %maximum_select_fusion), custom_call_target="InvertDiagBlocksLowerTriangular" | custom-call | tf_op jit(solution)/shard_map/triangular_solve | solution.py:80
  375.4 1.0 fusion.4
  376.5 1.0 fusion.22
  377.5 0.8 pad_maximum_fusion
  (18 shorter events, 0.4 us)
Async XLA Ops:
  7.2 42.0 %all-gather.4.cloned.1.call-start = ((), (), s32[]{:S(2)}) async-start(), calls=%async_computation | async-start | bytes 4718592 | tf_op jit(solution)/shard_map/all_gather | solution.py:25
  7.9 157.5 %all-gather.6.cloned.1.call-start = ((), (), s32[]{:S(2)}) async-start(), calls=%async_computation.1 | async-start | bytes 2621440 | tf_op jit(solution)/shard_map/all_gather | solution.py:38
  69.0 31.7 %copy-start = (f32[1,4,80,256,32]{3,4,2,1,0:T(8,128)S(1)}, f32[1,4,80,256,32]{3,4,2,1,0:T(8,128)}, u32[]{:S(2)}) copy-start(f32[1,4,80,256,32]{3,4,2,1,0:T(8,128)} %param.6) | copy-start | bytes 31457284
  168.3 1.3 collective-permute-start
  169.6 4.3 %collective-permute-start.1 = (f32[128,128]{0,1:T(8,128)S(1)}, f32[128,128]{0,1:T(8,128)S(1)}, u32[]{:S(2)}, u32[]{:S(2)}) collective-permute-start(f32[128,128]{0,1:T(8,128)S(1)} %fusion.30), channel_id=1, source_target_pairs={{0,2},{1,3},{2,0},{3,1},{4,6},{5,7},{6,4},{7,5},{8,10},{9,11},{10,... | collective-permute-start | bytes 196616 | tf_op jit(solution)/shard_map/ppermute | solution.py:12
  174.0 4.3 %collective-permute-start.2 = (f32[128,128]{0,1:T(8,128)S(1)}, f32[128,128]{0,1:T(8,128)S(1)}, u32[]{:S(2)}, u32[]{:S(2)}) collective-permute-start(f32[128,128]{0,1:T(8,128)S(1)} %fusion.31), channel_id=1, source_target_pairs={{0,4},{1,5},{2,6},{3,7},{4,0},{5,1},{6,2},{7,3},{8,12},{9,13},{10,... | collective-permute-start | bytes 196616 | tf_op jit(solution)/shard_map/ppermute | solution.py:12
Sparse Core Ops, SparseCore 0:
  9.9 39.2 all-gather.3
  119.7 45.6 all-gather.5
